TPU v7x, 512 devices: a whole 4x8x8 slice. The times are simulated.
512 devices in a mesh: rows: 32 (over x, z), cols: 16 (over y, core).
Axes of the slice: x: 4, y: 8, z: 8, core: 2. Of those that a mesh axis runs over, the one named last changes fastest.
Arguments:
- features: bfloat16 [768, 512, 2048], P(None, 'rows', 'cols'), may hold values from -6 to 6
- labels: int32 [512, 2048], P('rows', 'cols'), may hold values from 0 to 15
- w_input: bfloat16 [128, 768], replicated, may hold values from -0.21875 to 0.21875
- w_dilate4: bfloat16 [128, 1152], replicated, may hold values from -0.1875 to 0.1875
- w_dilate8: bfloat16 [128, 1152], replicated, may hold values from -0.1875 to 0.1875
- w_classes: bfloat16 [16, 128], replicated, may hold values from -0.5 to 0.5
Outputs:
- grad_input: float32 [128, 768], replicated
- grad_dilate4: float32 [128, 1152], replicated
- grad_dilate8: float32 [128, 1152], replicated
- grad_classes: float32 [16, 128], replicated
All inputs are finite; a program needn't handle non-finite values.
Results may differ from a plain program's by a relative error of at most 0.006.
Values may be sent and summed in bfloat16 or wider, within the bound.
No kernel may reach another device: no remote copies, remote signals or barrier semaphores. Data moves between devices by JAX's collectives and lax.ppermute only.
A program may use at most 128 MiB of HBM per device.

v0:
```python
import jax
import jax.numpy as jnp
from jax import lax
from jax.sharding import PartitionSpec as P

loss_weight = 0.03125


def extended(shard, sides, width):
    for axis, dim in sides:
        count, length = (lax.axis_size(axis), shard.shape[dim])
        up = [(i, (i + 1) % count) for i in range(count - 1)]
        down = [(j, i) for i, j in up]
        last = lax.slice_in_dim(shard, length - width, length, axis=dim)
        first = lax.slice_in_dim(shard, 0, width, axis=dim)
        before = lax.ppermute(last, axis, up)
        after = lax.ppermute(first, axis, down)
        shard = jnp.concatenate([before, shard, after], axis=dim)
    return shard


def smooth(value):
    return value * jax.nn.sigmoid(value)


def slope(value):
    sig = jax.nn.sigmoid(value)
    return sig * (1.0 + value * (1.0 - sig))


def gather_taps(padded, dilation, anchor, sign, out_rows, out_cols):
    pieces = []
    for tap in range(9):
        top = anchor + sign * (tap // 3 - 1) * dilation
        left = anchor + sign * (tap % 3 - 1) * dilation
        pieces.append(padded[:, top : top + out_rows, left : left + out_cols])
    stacked = jnp.concatenate(pieces, 0)
    return stacked.reshape(stacked.shape[0], out_rows * out_cols)


def pixel_contract(left, right):
    return lax.dot_general(
        left, right, (((1,), (1,)), ((), ())), preferred_element_type=jnp.float32
    )


def flipped(weight):
    chans = weight.shape[0]
    return weight.reshape(chans, 9, chans).transpose(2, 1, 0).reshape(chans, 9 * chans)


def local(features, labels, w_input, w_dilate4, w_dilate8, w_classes):
    chans = features.shape[0]
    rows = features.shape[1]
    cols = features.shape[2]
    pixels = rows * cols
    middle = w_input.shape[0]
    classes = w_classes.shape[0]
    flat = features.reshape(chans, pixels)
    a1 = jnp.dot(w_input, flat, preferred_element_type=jnp.float32)
    h1 = smooth(a1).astype(jnp.bfloat16).reshape(middle, rows, cols)
    h1_pad = extended(h1, (("rows", 1), ("cols", 2)), 4)
    a2 = jnp.dot(
        w_dilate4, gather_taps(h1_pad, 4, 4, 1, rows, cols), preferred_element_type=jnp.float32
    )
    h2 = smooth(a2).astype(jnp.bfloat16).reshape(middle, rows, cols)
    h2_pad = extended(h2, (("rows", 1), ("cols", 2)), 8)
    h2_taps = gather_taps(h2_pad, 8, 8, 1, rows, cols)
    a3 = jnp.dot(w_dilate8, h2_taps, preferred_element_type=jnp.float32)
    h3 = smooth(a3).astype(jnp.bfloat16)
    logits = jnp.dot(w_classes, h3, preferred_element_type=jnp.float32)
    expo = jnp.exp(logits)
    prob = expo / jnp.sum(expo, axis=0, keepdims=True)
    onehot = (labels.reshape(1, pixels) == jnp.arange(classes, dtype=jnp.int32)[:, None]).astype(
        jnp.float32
    )
    g4 = (loss_weight * (prob - onehot)).astype(jnp.bfloat16)
    grad_classes = pixel_contract(g4, h3)
    back3 = lax.dot_general(
        w_classes, g4, (((0,), (0,)), ((), ())), preferred_element_type=jnp.float32
    )
    g3 = (back3 * slope(a3)).astype(jnp.bfloat16)
    grad_dilate8 = pixel_contract(g3, h2_taps)
    g3_grid = g3.reshape(middle, rows, cols)
    g3_pad = extended(g3_grid, (("rows", 1), ("cols", 2)), 8)
    back2 = jnp.dot(
        flipped(w_dilate8),
        gather_taps(g3_pad, 8, 8, -1, rows, cols),
        preferred_element_type=jnp.float32,
    )
    g2 = (back2 * slope(a2)).astype(jnp.bfloat16)
    g2_grid = g2.reshape(middle, rows, cols)
    g2_pad = extended(g2_grid, (("rows", 1), ("cols", 2)), 4)
    grad_dilate4 = pixel_contract(g2, gather_taps(h1_pad, 4, 4, 1, rows, cols))
    back1 = jnp.dot(
        flipped(w_dilate4),
        gather_taps(g2_pad, 4, 4, -1, rows, cols),
        preferred_element_type=jnp.float32,
    )
    g1 = (back1 * slope(a1)).astype(jnp.bfloat16)
    grad_input = pixel_contract(g1, flat)
    grad_input, grad_dilate4, grad_dilate8, grad_classes = lax.psum(
        (grad_input, grad_dilate4, grad_dilate8, grad_classes), ("rows", "cols")
    )
    return (grad_input, grad_dilate4, grad_dilate8, grad_classes)


def solution(mesh):
    return jax.shard_map(
        local,
        mesh=mesh,
        in_specs=(P(None, "rows", "cols"), P("rows", "cols"), P(), P(), P(), P()),
        out_specs=(P(), P(), P(), P()),
        check_vma=False,
    )
```

profile of v0, /device:TPU:17, one launch (start us, length us, event | category | flops | bytes accessed | tf_op | source)
XLA Modules:
  0.0 527.5 jit_solution(8724425826203877093)
XLA Ops:
  8.1 2.5 fusion.2
  11.9 4.0 collective-permute-start
  18.1 4.7 collective-permute-done.1
  22.9 4.6 collective-permute-start.2
  27.5 1.9 collective-permute-start.3
  33.1 1.8 fusion.27
  34.9 2.5 copy.25
  37.4 2.0 bitcast_dynamic-update-slice_fusion.19
  39.3 2.5 copy.27
  41.8 2.5 copy.28
  45.2 1.9 bitcast_dynamic-update-slice_fusion.17
  47.2 1.9 bitcast_dynamic-update-slice_fusion.16
  50.2 1.7 copy.29
  55.1 2.0 bitcast_dynamic-update-slice_fusion.14
  59.0 3.3 convolution_bitcast_fusion.1
  64.0 4.7 collective-permute-start.4
  70.1 1.8 copy.72
  72.0 1.8 copy.58
  73.8 1.9 copy.59
  75.7 1.8 copy.73
  77.6 1.9 collective-permute-done.5
  80.2 3.8 collective-permute-start.6
  84.0 1.9 collective-permute-start.7
  85.9 1.8 copy.38
  87.7 1.8 copy.43
  89.6 2.2 pad_maximum_fusion.8
  91.8 2.4 pad_maximum_fusion
  95.4 2.1 copy.80
  97.5 1.9 constant_dynamic-update-slice_fusion.7
  103.1 2.0 bitcast_dynamic-update-slice_fusion.11
  109.1 2.0 copy.84
  113.2 1.9 constant_dynamic-update-slice_fusion.2
  115.1 1.9 bitcast_dynamic-update-slice_fusion.10
  117.8 3.4 multiply_convert_fusion
  125.8 5.2 collective-permute-start.8
  131.0 4.8 fusion.35
  136.5 3.3 collective-permute-start.10
  139.9 3.6 collective-permute-start.11
  145.8 2.3 pad_maximum_fusion.6
  148.0 2.4 maximum_maximum_fusion.1
  151.6 2.1 copy.86
  153.7 1.9 constant_dynamic-update-slice_fusion.14
  156.8 2.1 copy.87
  160.2 2.0 bitcast_dynamic-update-slice_fusion.9
  162.1 1.9 constant_dynamic-update-slice_fusion.13
  166.9 2.0 copy.90
  171.1 1.9 constant_dynamic-update-slice_fusion.9
  172.9 1.9 bitcast_dynamic-update-slice_fusion.8
  175.7 3.5 fusion.11
  181.5 4.7 collective-permute-start.12
  186.2 4.8 fusion.34
  191.0 1.9 collective-permute-start.14
  193.0 3.9 collective-permute-start.15
  204.1 1.7 copy.67
  205.8 2.0 bitcast_dynamic-update-slice_fusion.6
  210.5 1.7 copy.68
  212.2 1.7 copy.69
  214.0 1.7 copy.71
  219.3 6.2 %fusion = f32[128,768]{1,0:T(8,128)} fusion(bf16[96,8,16,128]{3,2,1,0:T(8,128)(2,1)} %bitcast.157, bf16[1152,2048]{1,0:T(8,128)(2,1)} %bitcast_dynamic-update-slice_fusion, bf16[128,1152]{0,1:T(8,128)(2,1)} %bitcast.192, f32[128,2048]{1,0:T(8,128)S(1)} %fusion.2), kind=kOutput, calls=%fused_computation | convolution fusion | flops 1008992256 | bytes 9601024 | tf_op jit(solution)/shard_map/dot_general | solution.py:42
  225.8 106.8 %psum.31 = f32[16,128]{1,0:T(8,128)} all-reduce(f32[16,128]{1,0:T(8,128)S(1)} %fusion.16), channel_id=1, replica_groups=mesh['rows'=32,'cols'=16] {'rows','cols'}, use_global_device_ids=true, to_apply=%region_4.0 | all-reduce | flops 2048 | bytes 16384 | tf_op jit(solution)/shard_map/psum | solution.py:102
  332.6 182.4 %all-reduce.3.cloned.1.call-done = (f32[128,768]{1,0:T(8,128)}, f32[128,1152]{1,0:T(8,128)}, f32[128,1152]{1,0:T(8,128)}) async-done(((f32[128,768]{1,0:T(8,128)}, f32[128,1152]{1,0:T(8,128)}, f32[128,1152]{1,0:T(8,128)}), (f32[128,768]{1,0:T(8,128)}, f32[128,1152]{1,0:T(8,128)}, f32[128,1152]{1,0:T(8,128)})) %all-reduce.3.cloned.1.call-update) | async-done | bytes 1572880 | tf_op jit(solution)/shard_map/psum | solution.py:102
  515.0 1.8 copy.180
  516.8 1.9 copy.181
  518.7 1.9 copy.182
  (120 shorter events, 63.7 us)
Async XLA Ops:
  7.2 0.9 copy-start
  7.2 507.8 %all-reduce.3.cloned.1.call-start = ((), (), s32[]{:S(2)}) async-start(), calls=%async_computation | async-start | bytes 3145728 | tf_op jit(solution)/shard_map/psum | solution.py:102
  11.9 6.2 %collective-permute-start = (bf16[128,4,128]{0,1,2:T(4,128)(2,1)S(1)}, bf16[128,4,128]{0,1,2:T(4,128)(2,1)S(1)}, u32[]{:S(2)}, u32[]{:S(2)}) collective-permute-start(bf16[128,4,128]{0,1,2:T(4,128)(2,1)S(1)} %get-tuple-element.61), channel_id=1, source_target_pairs={{0,16},{16,32},{32,48},{48,64},{64,80},{80,96},{96,112},{112,128},... | collective-permute-start | bytes 393224 | tf_op jit(solution)/shard_map/ppermute | solution.py:16
  15.9 6.9 %collective-permute-start.1 = (bf16[128,4,128]{0,1,2:T(4,128)(2,1)S(1)}, bf16[128,4,128]{0,1,2:T(4,128)(2,1)S(1)}, u32[]{:S(2)}, u32[]{:S(2)}) collective-permute-start(bf16[128,4,128]{0,1,2:T(4,128)(2,1)S(1)} %get-tuple-element.62), channel_id=1, source_target_pairs={{16,0},{32,16},{48,32},{64,48},{80,64},{96,80},{112,96},{128,112},... | collective-permute-start | bytes 393224 | tf_op jit(solution)/shard_map/ppermute | solution.py:17
  22.9 9.6 %collective-permute-start.2 = (bf16[128,24,4]{0,1,2:T(8,128)(2,1)S(1)}, bf16[128,24,4]{0,1,2:T(8,128)(2,1)S(1)}, u32[]{:S(2)}, u32[]{:S(2)}) collective-permute-start(bf16[128,24,4]{0,1,2:T(8,128)(2,1)S(1)} %get-tuple-element.46), channel_id=1, source_target_pairs={{0,1},{1,2},{2,3},{3,4},{4,5},{5,6},{6,7},{7,8},{8,9},{9,10},{10,1... | collective-permute-start | bytes 73736 | tf_op jit(solution)/shard_map/ppermute | solution.py:16
  27.5 5.1 collective-permute-start.3
  64.0 13.6 %collective-permute-start.4 = (bf16[128,8,128]{0,2,1:T(8,128)(2,1)}, bf16[128,8,128]{0,2,1:T(8,128)(2,1)}, u32[]{:S(2)}, u32[]{:S(2)}) collective-permute-start(bf16[128,8,128]{0,2,1:T(8,128)(2,1)} %get-tuple-element.57), channel_id=1, source_target_pairs={{0,16},{16,32},{32,48},{48,64},{64,80},{80,96},{96,112},{112,128},... | collective-permute-start | bytes 786440 | tf_op jit(solution)/shard_map/ppermute | solution.py:16
  68.7 10.8 %collective-permute-start.5 = (bf16[128,8,128]{0,2,1:T(8,128)(2,1)}, bf16[128,8,128]{0,2,1:T(8,128)(2,1)}, u32[]{:S(2)}, u32[]{:S(2)}) collective-permute-start(bf16[128,8,128]{0,2,1:T(8,128)(2,1)} %get-tuple-element.58), channel_id=1, source_target_pairs={{16,0},{32,16},{48,32},{64,48},{80,64},{96,80},{112,96},{128,112},... | collective-permute-start | bytes 786440 | tf_op jit(solution)/shard_map/ppermute | solution.py:17
  80.2 11.5 %collective-permute-start.6 = (bf16[128,32,8]{0,2,1:T(8,128)(2,1)S(1)}, bf16[128,32,8]{0,2,1:T(8,128)(2,1)S(1)}, u32[]{:S(2)}, u32[]{:S(2)}) collective-permute-start(bf16[128,32,8]{0,2,1:T(8,128)(2,1)S(1)} %get-tuple-element.26), channel_id=1, source_target_pairs={{0,1},{1,2},{2,3},{3,4},{4,5},{5,6},{6,7},{7,8},{8,9},{9,10},{10,1... | collective-permute-start | bytes 196616 | tf_op jit(solution)/shard_map/ppermute | solution.py:16
  84.0 7.8 %collective-permute-start.7 = (bf16[128,32,8]{0,2,1:T(8,128)(2,1)S(1)}, bf16[128,32,8]{0,2,1:T(8,128)(2,1)S(1)}, u32[]{:S(2)}, u32[]{:S(2)}) collective-permute-start(bf16[128,32,8]{0,2,1:T(8,128)(2,1)S(1)} %get-tuple-element.25), channel_id=1, source_target_pairs={{1,0},{2,1},{3,2},{4,3},{5,4},{6,5},{7,6},{8,7},{9,8},{10,9},{11,1... | collective-permute-start | bytes 196616 | tf_op jit(solution)/shard_map/ppermute | solution.py:17
  94.2 5.2 copy-start.2
  117.8 3.4 copy-start.13
  117.8 3.6 copy-start.14
  121.2 1.7 copy-start.11
  122.0 13.9 %copy-start.6 = (bf16[128,2048]{1,0:T(8,128)(2,1)}, bf16[128,2048]{1,0:T(8,128)(2,1)S(1)}, u32[]{:S(2)}) copy-start(bf16[128,2048]{1,0:T(8,128)(2,1)S(1)} %fusion.9) | copy-start | bytes 1572868
  124.5 11.3 %collective-permute-start.9 = (bf16[128,8,128]{0,2,1:T(8,128)(2,1)S(1)}, bf16[128,8,128]{0,2,1:T(8,128)(2,1)S(1)}, u32[]{:S(2)}, u32[]{:S(2)}) collective-permute-start(bf16[128,8,128]{0,2,1:T(8,128)(2,1)S(1)} %get-tuple-element.54), channel_id=1, source_target_pairs={{16,0},{32,16},{48,32},{64,48},{80,64},{96,80},{112,96},{128,112},... | collective-permute-start | bytes 786440 | tf_op jit(solution)/shard_map/ppermute | solution.py:17
  125.8 10.0 %collective-permute-start.8 = (bf16[128,8,128]{0,2,1:T(8,128)(2,1)S(1)}, bf16[128,8,128]{0,2,1:T(8,128)(2,1)S(1)}, u32[]{:S(2)}, u32[]{:S(2)}) collective-permute-start(bf16[128,8,128]{0,2,1:T(8,128)(2,1)S(1)} %get-tuple-element.53), channel_id=1, source_target_pairs={{0,16},{16,32},{32,48},{48,64},{64,80},{80,96},{96,112},{112,128},... | collective-permute-start | bytes 786440 | tf_op jit(solution)/shard_map/ppermute | solution.py:16
  135.8 0.7 copy-start.8
  135.8 4.1 copy-start.9
  136.5 11.5 %collective-permute-start.10 = (bf16[128,32,8]{0,2,1:T(8,128)(2,1)S(1)}, bf16[128,32,8]{0,2,1:T(8,128)(2,1)S(1)}, u32[]{:S(2)}, u32[]{:S(2)}) collective-permute-start(bf16[128,32,8]{0,2,1:T(8,128)(2,1)S(1)} %get-tuple-element.22), channel_id=1, source_target_pairs={{1,0},{2,1},{3,2},{4,3},{5,4},{6,5},{7,6},{8,7},{9,8},{10,9},{11,1... | collective-permute-start | bytes 196616 | tf_op jit(solution)/shard_map/ppermute | solution.py:17
  139.9 8.2 %collective-permute-start.11 = (bf16[128,32,8]{0,2,1:T(8,128)(2,1)S(1)}, bf16[128,32,8]{0,2,1:T(8,128)(2,1)S(1)}, u32[]{:S(2)}, u32[]{:S(2)}) collective-permute-start(bf16[128,32,8]{0,2,1:T(8,128)(2,1)S(1)} %get-tuple-element.21), channel_id=1, source_target_pairs={{0,1},{1,2},{2,3},{3,4},{4,5},{5,6},{6,7},{7,8},{8,9},{9,10},{10,1... | collective-permute-start | bytes 196616 | tf_op jit(solution)/shard_map/ppermute | solution.py:16
  150.4 5.1 copy-start.3
  156.8 8.1 %copy-start.7 = (bf16[128,2048]{1,0:T(8,128)(2,1)S(1)}, bf16[128,2048]{1,0:T(8,128)(2,1)}, u32[]{:S(2)}) copy-start(bf16[128,2048]{1,0:T(8,128)(2,1)} %copy-done.6) | copy-start | bytes 1572868
  179.2 17.8 %copy-start.4 = (bf16[128,2048]{1,0:T(8,128)(2,1)}, bf16[128,2048]{1,0:T(8,128)(2,1)S(1)}, u32[]{:S(2)}) copy-start(bf16[128,2048]{1,0:T(8,128)(2,1)S(1)} %fusion.11) | copy-start | bytes 1572868
  180.2 10.8 %collective-permute-start.13 = (bf16[128,4,128]{0,1,2:T(4,128)(2,1)S(1)}, bf16[128,4,128]{0,1,2:T(4,128)(2,1)S(1)}, u32[]{:S(2)}, u32[]{:S(2)}) collective-permute-start(bf16[128,4,128]{0,1,2:T(4,128)(2,1)S(1)} %get-tuple-element.50), channel_id=1, source_target_pairs={{16,0},{32,16},{48,32},{64,48},{80,64},{96,80},{112,96},{128,112},... | collective-permute-start | bytes 393224 | tf_op jit(solution)/shard_map/ppermute | solution.py:17
  181.5 9.5 %collective-permute-start.12 = (bf16[128,4,128]{0,1,2:T(4,128)(2,1)S(1)}, bf16[128,4,128]{0,1,2:T(4,128)(2,1)S(1)}, u32[]{:S(2)}, u32[]{:S(2)}) collective-permute-start(bf16[128,4,128]{0,1,2:T(4,128)(2,1)S(1)} %get-tuple-element.49), channel_id=1, source_target_pairs={{0,16},{16,32},{32,48},{48,64},{64,80},{80,96},{96,112},{112,128},... | collective-permute-start | bytes 393224 | tf_op jit(solution)/shard_map/ppermute | solution.py:16
  191.0 7.7 %collective-permute-start.14 = (bf16[128,24,4]{0,1,2:T(8,128)(2,1)S(1)}, bf16[128,24,4]{0,1,2:T(8,128)(2,1)S(1)}, u32[]{:S(2)}, u32[]{:S(2)}) collective-permute-start(bf16[128,24,4]{0,1,2:T(8,128)(2,1)S(1)} %get-tuple-element.42), channel_id=1, source_target_pairs={{1,0},{2,1},{3,2},{4,3},{5,4},{6,5},{7,6},{8,7},{9,8},{10,9},{11,1... | collective-permute-start | bytes 73736 | tf_op jit(solution)/shard_map/ppermute | solution.py:17
  193.0 5.7 %collective-permute-start.15 = (bf16[128,24,4]{0,1,2:T(8,128)(2,1)S(1)}, bf16[128,24,4]{0,1,2:T(8,128)(2,1)S(1)}, u32[]{:S(2)}, u32[]{:S(2)}) collective-permute-start(bf16[128,24,4]{0,1,2:T(8,128)(2,1)S(1)} %get-tuple-element.41), channel_id=1, source_target_pairs={{0,1},{1,2},{2,3},{3,4},{4,5},{5,6},{6,7},{7,8},{8,9},{9,10},{10,1... | collective-permute-start | bytes 73736 | tf_op jit(solution)/shard_map/ppermute | solution.py:16
  201.1 8.5 %copy-start.5 = (bf16[128,2048]{1,0:T(8,128)(2,1)S(1)}, bf16[128,2048]{1,0:T(8,128)(2,1)}, u32[]{:S(2)}) copy-start(bf16[128,2048]{1,0:T(8,128)(2,1)} %copy-done.4) | copy-start | bytes 1572868
  205.8 11.7 %copy-start.10 = (bf16[128,16,128]{2,1,0:T(8,128)(2,1)S(1)}, bf16[128,16,128]{2,1,0:T(8,128)(2,1)}, u32[]{:S(2)}) copy-start(bf16[128,16,128]{2,1,0:T(8,128)(2,1)} %get-tuple-element.47) | copy-start | bytes 1572868
  219.3 6.2 %copy-start.12 = (bf16[128,2048]{1,0:T(8,128)(2,1)S(1)}, bf16[128,2048]{1,0:T(8,128)(2,1)}, u32[]{:S(2)}) copy-start(bf16[128,2048]{1,0:T(8,128)(2,1)} %copy-done.11) | copy-start | bytes 1572868
  219.3 301.3 %copy-start.1 = (bf16[128,768]{1,0:T(8,128)(2,1)S(1)}, bf16[128,768]{1,0:T(8,128)(2,1)}, u32[]{:S(2)}) copy-start(bf16[128,768]{1,0:T(8,128)(2,1)} %param.8) | copy-start | bytes 589828
Sparse Core Ops, SparseCore 0:
  225.7 289.2 all-reduce.2
where the time goes:
time: 530 us; the launch traced here: 527 us
  waiting for transfers between devices  190 us (36%)
  local copies, waits for them, and re-layouts  121 us (23%)
  blocking collectives  107 us (20%)
  starting transfers between devices  49 us (9%)
  matrix products  29.4 us (6%)
  other arithmetic  16.8 us (3%)
  between operations  14.6 us (3%)
    psum x1, waiting for transfers between devices, local(): lax.psum((grad_input, grad_dilate4, grad_dilate8, grad_classes), ('rows',...  182 us
    psum x1, blocking collectives, local(): lax.psum((grad_input, grad_dilate4, grad_dilate8, grad_classes), ('rows',...  107 us
    unnamed x69, local copies, waits for them, and re-layouts  53.3 us
    ppermute x8, starting transfers between devices, extended(): before = lax.ppermute(last, axis, up)  34.5 us
    slice x19, local copies, waits for them, and re-layouts, gather_taps(): pieces.append(padded[:, top:top + out_rows, left:left + out_cols])  28.9 us
    concatenate x16, local copies, waits for them, and re-layouts, gather_taps(): stacked = jnp.concatenate(pieces, 0)  22.5 us
    dot_general x4, matrix products, pixel_contract(): lax.dot_general(left, right, (((1,), (1,)), ((), ())), preferred_element_...  16 us
    ppermute x8, starting transfers between devices, extended(): after = lax.ppermute(first, axis, down)  14.4 us
  transfers between devices with their start and end apart: 17, of which 5 were waited for; matrix products, arithmetic and copies ran while one was open for 6% of the time, Pallas kernels for 0%

commit v1 on v0

--- a/solution.py
+++ b/solution.py
@@ -100,7 +100,7 @@
     g1 = (back1 * slope(a1)).astype(jnp.bfloat16)
     grad_input = pixel_contract(g1, flat)
     grad_input, grad_dilate4, grad_dilate8, grad_classes = lax.psum(
-        (grad_input, grad_dilate4, grad_dilate8, grad_classes), ("rows", "cols")
+        lax.psum((grad_input, grad_dilate4, grad_dilate8, grad_classes), "cols"), "rows"
     )
     return (grad_input, grad_dilate4, grad_dilate8, grad_classes)
 

time: 530 us -> 540 us (1.019)
  the two profiles are of different devices: /device:TPU:17 before, /device:TPU:8 now
where the time goes in v1:
time: 540 us; the launch traced here: 537 us
  waiting for transfers between devices  204 us (38%)
  local copies, waits for them, and re-layouts  123 us (23%)
  blocking collectives  103 us (19%)
  starting transfers between devices  45.7 us (8%)
  matrix products  29.4 us (5%)
  other arithmetic  16.7 us (3%)
  between operations  14.6 us (3%)
    psum x1, waiting for transfers between devices, local(): lax.psum((grad_input, grad_dilate4, grad_dilate8, grad_classes), 'cols')  126 us
    psum x1, blocking collectives, local(): lax.psum(lax.psum((grad_input, grad_dilate4, grad_dilate8, grad_classes),...  77.5 us
    psum x1, waiting for transfers between devices, local(): lax.psum(lax.psum((grad_input, grad_dilate4, grad_dilate8, grad_classes),...  67.8 us
    unnamed x65, local copies, waits for them, and re-layouts  53.8 us
    slice x19, local copies, waits for them, and re-layouts, gather_taps(): pieces.append(padded[:, top:top + out_rows, left:left + out_cols])  31.1 us
    ppermute x8, starting transfers between devices, extended(): before = lax.ppermute(last, axis, up)  28.2 us
    psum x1, blocking collectives, local(): lax.psum((grad_input, grad_dilate4, grad_dilate8, grad_classes), 'cols')  25.6 us
    concatenate x16, local copies, waits for them, and re-layouts, gather_taps(): stacked = jnp.concatenate(pieces, 0)  22.5 us
  transfers between devices with their start and end apart: 18, of which 7 were waited for; matrix products, arithmetic and copies ran while one was open for 6% of the time, Pallas kernels for 0%

profile of v1, /device:TPU:8, one launch (start us, length us, event | category | flops | bytes accessed | tf_op | source)
XLA Modules:
  0.0 537.3 jit_solution(17810469706531158690)
XLA Ops:
  8.1 2.5 fusion.2
  11.9 4.3 collective-permute-start
  18.9 4.8 collective-permute-done.1
  23.7 1.9 collective-permute-start.2
  25.6 3.6 collective-permute-start.3
  32.8 1.8 fusion.27
  34.6 2.5 copy.25
  37.1 2.0 bitcast_dynamic-update-slice_fusion.19
  39.1 2.5 copy.27
  41.6 2.5 copy.28
  45.0 1.9 bitcast_dynamic-update-slice_fusion.17
  47.0 1.9 bitcast_dynamic-update-slice_fusion.16
  54.9 2.0 bitcast_dynamic-update-slice_fusion.14
  58.7 3.3 convolution_bitcast_fusion.1
  63.8 5.0 collective-permute-start.4
  70.2 1.8 copy.72
  72.1 1.8 copy.58
  73.9 1.9 copy.59
  75.8 1.8 copy.73
  77.6 2.5 collective-permute-done.5
  80.9 1.9 collective-permute-start.6
  82.8 3.6 collective-permute-start.7
  86.5 1.8 copy.38
  88.3 1.8 copy.43
  90.1 2.2 pad_maximum_fusion.8
  92.3 2.4 pad_maximum_fusion
  95.9 2.1 copy.80
  98.0 1.9 constant_dynamic-update-slice_fusion.7
  103.6 2.0 bitcast_dynamic-update-slice_fusion.11
  109.6 2.0 copy.84
  113.8 1.9 constant_dynamic-update-slice_fusion.2
  115.7 1.9 bitcast_dynamic-update-slice_fusion.10
  118.5 3.4 multiply_convert_fusion
  126.4 5.5 %collective-permute-start.8 = (bf16[128,8,128]{0,2,1:T(8,128)(2,1)S(1)}, bf16[128,8,128]{0,2,1:T(8,128)(2,1)S(1)}, u32[]{:S(2)}, u32[]{:S(2)}) collective-permute-start(bf16[128,8,128]{0,2,1:T(8,128)(2,1)S(1)} %get-tuple-element.56), channel_id=1, source_target_pairs={{0,16},{16,32},{32,48},{48,64},{64,80},{80,96},{96,112},{112,128},... | collective-permute-start | bytes 786440 | tf_op jit(solution)/shard_map/ppermute | solution.py:16
  131.9 4.8 fusion.35
  137.6 1.9 collective-permute-start.10
  139.5 2.4 collective-permute-start.11
  144.2 2.3 pad_maximum_fusion.6
  146.5 2.4 maximum_maximum_fusion.1
  150.1 2.0 copy.86
  152.2 1.9 constant_dynamic-update-slice_fusion.14
  155.3 2.1 copy.87
  158.6 2.0 bitcast_dynamic-update-slice_fusion.9
  160.6 1.9 constant_dynamic-update-slice_fusion.13
  165.5 2.0 copy.90
  169.6 1.9 constant_dynamic-update-slice_fusion.9
  171.5 1.9 bitcast_dynamic-update-slice_fusion.8
  174.3 3.5 fusion.11
  180.0 5.0 collective-permute-start.12
  185.1 4.8 fusion.34
  189.9 2.9 collective-permute-start.14
  192.7 2.1 collective-permute-start.15
  207.1 2.0 bitcast_dynamic-update-slice_fusion.6
  209.1 2.0 bitcast_dynamic-update-slice_fusion.5
  214.5 1.7 copy.69
  216.3 1.7 copy.71
  221.6 6.2 %fusion = f32[128,768]{1,0:T(8,128)} fusion(bf16[96,8,16,128]{3,2,1,0:T(8,128)(2,1)} %bitcast.157, bf16[1152,2048]{1,0:T(8,128)(2,1)} %bitcast_dynamic-update-slice_fusion, bf16[128,1152]{0,1:T(8,128)(2,1)} %bitcast.192, f32[128,2048]{1,0:T(8,128)S(1)} %fusion.2), kind=kOutput, calls=%fused_computation | convolution fusion | flops 1008992256 | bytes 9601024 | tf_op jit(solution)/shard_map/dot_general | solution.py:42
  227.9 125.8 %all-reduce.7.cloned.1.call-done = (f32[128,768]{1,0:T(8,128)}, f32[128,1152]{1,0:T(8,128)}, f32[128,1152]{1,0:T(8,128)}) async-done(((f32[128,768]{1,0:T(8,128)}, f32[128,1152]{1,0:T(8,128)}, f32[128,1152]{1,0:T(8,128)}), (f32[128,768]{1,0:T(8,128)}, f32[128,1152]{1,0:T(8,128)}, f32[128,1152]{1,0:T(8,128)})) %all-reduce.7.cloned.1.call-update) | async-done | bytes 1572880 | tf_op jit(solution)/shard_map/psum | solution.py:103
  354.0 25.6 %psum.62 = f32[16,128]{1,0:T(8,128)S(1)} all-reduce(f32[16,128]{1,0:T(8,128)S(1)} %fusion.16), channel_id=1, replica_groups=mesh['rows'=32,'cols'=16] {'cols'}, use_global_device_ids=true, to_apply=%region_7.0 | all-reduce | flops 2048 | bytes 16384 | tf_op jit(solution)/shard_map/psum | solution.py:103
  379.6 77.5 %psum.63 = f32[16,128]{1,0:T(8,128)} all-reduce(f32[16,128]{1,0:T(8,128)S(1)} %psum.62), channel_id=1, replica_groups=mesh['rows'=32,'cols'=16] {'rows'}, use_global_device_ids=true, to_apply=%region_8.0 | all-reduce | flops 2048 | bytes 16384 | tf_op jit(solution)/shard_map/psum | solution.py:102
  457.0 67.8 %all-reduce.5.cloned.1.call-done = (f32[128,768]{1,0:T(8,128)}, f32[128,1152]{1,0:T(8,128)}, f32[128,1152]{1,0:T(8,128)}) async-done(((f32[128,768]{1,0:T(8,128)}, f32[128,1152]{1,0:T(8,128)}, f32[128,1152]{1,0:T(8,128)}), (f32[128,768]{1,0:T(8,128)}, f32[128,1152]{1,0:T(8,128)}, f32[128,1152]{1,0:T(8,128)})) %all-reduce.5.cloned.1.call-update) | async-done | bytes 1572880 | tf_op jit(solution)/shard_map/psum | solution.py:102
  524.9 1.8 copy.183
  526.7 1.9 copy.184
  528.6 1.9 copy.185
  (120 shorter events, 72.1 us)
Async XLA Ops:
  7.2 0.9 copy-start
  7.2 346.5 %all-reduce.7.cloned.1.call-start = ((), (), s32[]{:S(2)}) async-start(), calls=%async_computation.1 | async-start | bytes 3145728 | tf_op jit(solution)/shard_map/psum | solution.py:103
  11.9 7.0 %collective-permute-start = (bf16[128,4,128]{0,1,2:T(4,128)(2,1)S(1)}, bf16[128,4,128]{0,1,2:T(4,128)(2,1)S(1)}, u32[]{:S(2)}, u32[]{:S(2)}) collective-permute-start(bf16[128,4,128]{0,1,2:T(4,128)(2,1)S(1)} %get-tuple-element.64), channel_id=1, source_target_pairs={{0,16},{16,32},{32,48},{48,64},{64,80},{80,96},{96,112},{112,128},... | collective-permute-start | bytes 393224 | tf_op jit(solution)/shard_map/ppermute | solution.py:16
  16.2 7.5 %collective-permute-start.1 = (bf16[128,4,128]{0,1,2:T(4,128)(2,1)S(1)}, bf16[128,4,128]{0,1,2:T(4,128)(2,1)S(1)}, u32[]{:S(2)}, u32[]{:S(2)}) collective-permute-start(bf16[128,4,128]{0,1,2:T(4,128)(2,1)S(1)} %get-tuple-element.65), channel_id=1, source_target_pairs={{16,0},{32,16},{48,32},{64,48},{80,64},{96,80},{112,96},{128,112},... | collective-permute-start | bytes 393224 | tf_op jit(solution)/shard_map/ppermute | solution.py:17
  23.7 8.7 %collective-permute-start.2 = (bf16[128,24,4]{0,1,2:T(8,128)(2,1)S(1)}, bf16[128,24,4]{0,1,2:T(8,128)(2,1)S(1)}, u32[]{:S(2)}, u32[]{:S(2)}) collective-permute-start(bf16[128,24,4]{0,1,2:T(8,128)(2,1)S(1)} %get-tuple-element.49), channel_id=1, source_target_pairs={{0,1},{1,2},{2,3},{3,4},{4,5},{5,6},{6,7},{7,8},{8,9},{9,10},{10,1... | collective-permute-start | bytes 73736 | tf_op jit(solution)/shard_map/ppermute | solution.py:16
  25.6 6.7 %collective-permute-start.3 = (bf16[128,24,4]{0,1,2:T(8,128)(2,1)S(1)}, bf16[128,24,4]{0,1,2:T(8,128)(2,1)S(1)}, u32[]{:S(2)}, u32[]{:S(2)}) collective-permute-start(bf16[128,24,4]{0,1,2:T(8,128)(2,1)S(1)} %get-tuple-element.48), channel_id=1, source_target_pairs={{1,0},{2,1},{3,2},{4,3},{5,4},{6,5},{7,6},{8,7},{9,8},{10,9},{11,1... | collective-permute-start | bytes 73736 | tf_op jit(solution)/shard_map/ppermute | solution.py:17
  63.8 13.8 %collective-permute-start.4 = (bf16[128,8,128]{0,2,1:T(8,128)(2,1)}, bf16[128,8,128]{0,2,1:T(8,128)(2,1)}, u32[]{:S(2)}, u32[]{:S(2)}) collective-permute-start(bf16[128,8,128]{0,2,1:T(8,128)(2,1)} %get-tuple-element.60), channel_id=1, source_target_pairs={{0,16},{16,32},{32,48},{48,64},{64,80},{80,96},{96,112},{112,128},... | collective-permute-start | bytes 786440 | tf_op jit(solution)/shard_map/ppermute | solution.py:16
  68.7 11.4 %collective-permute-start.5 = (bf16[128,8,128]{0,2,1:T(8,128)(2,1)}, bf16[128,8,128]{0,2,1:T(8,128)(2,1)}, u32[]{:S(2)}, u32[]{:S(2)}) collective-permute-start(bf16[128,8,128]{0,2,1:T(8,128)(2,1)} %get-tuple-element.61), channel_id=1, source_target_pairs={{16,0},{32,16},{48,32},{64,48},{80,64},{96,80},{112,96},{128,112},... | collective-permute-start | bytes 786440 | tf_op jit(solution)/shard_map/ppermute | solution.py:17
  80.9 11.4 %collective-permute-start.6 = (bf16[128,32,8]{0,2,1:T(8,128)(2,1)S(1)}, bf16[128,32,8]{0,2,1:T(8,128)(2,1)S(1)}, u32[]{:S(2)}, u32[]{:S(2)}) collective-permute-start(bf16[128,32,8]{0,2,1:T(8,128)(2,1)S(1)} %get-tuple-element.29), channel_id=1, source_target_pairs={{0,1},{1,2},{2,3},{3,4},{4,5},{5,6},{6,7},{7,8},{8,9},{9,10},{10,1... | collective-permute-start | bytes 196616 | tf_op jit(solution)/shard_map/ppermute | solution.py:16
  82.8 9.5 %collective-permute-start.7 = (bf16[128,32,8]{0,2,1:T(8,128)(2,1)S(1)}, bf16[128,32,8]{0,2,1:T(8,128)(2,1)S(1)}, u32[]{:S(2)}, u32[]{:S(2)}) collective-permute-start(bf16[128,32,8]{0,2,1:T(8,128)(2,1)S(1)} %get-tuple-element.28), channel_id=1, source_target_pairs={{1,0},{2,1},{3,2},{4,3},{5,4},{6,5},{7,6},{8,7},{9,8},{10,9},{11,1... | collective-permute-start | bytes 196616 | tf_op jit(solution)/shard_map/ppermute | solution.py:17
  94.7 5.2 copy-start.2
  118.5 3.4 copy-start.11
  118.5 3.6 copy-start.12
  121.8 1.7 copy-start.9
  122.6 15.0 %copy-start.4 = (bf16[128,2048]{1,0:T(8,128)(2,1)}, bf16[128,2048]{1,0:T(8,128)(2,1)S(1)}, u32[]{:S(2)}) copy-start(bf16[128,2048]{1,0:T(8,128)(2,1)S(1)} %fusion.9) | copy-start | bytes 1572868
  125.1 11.6 %collective-permute-start.9 = (bf16[128,8,128]{0,2,1:T(8,128)(2,1)S(1)}, bf16[128,8,128]{0,2,1:T(8,128)(2,1)S(1)}, u32[]{:S(2)}, u32[]{:S(2)}) collective-permute-start(bf16[128,8,128]{0,2,1:T(8,128)(2,1)S(1)} %get-tuple-element.57), channel_id=1, source_target_pairs={{16,0},{32,16},{48,32},{64,48},{80,64},{96,80},{112,96},{128,112},... | collective-permute-start | bytes 786440 | tf_op jit(solution)/shard_map/ppermute | solution.py:17
  126.4 11.2 %collective-permute-start.8 = (bf16[128,8,128]{0,2,1:T(8,128)(2,1)S(1)}, bf16[128,8,128]{0,2,1:T(8,128)(2,1)S(1)}, u32[]{:S(2)}, u32[]{:S(2)}) collective-permute-start(bf16[128,8,128]{0,2,1:T(8,128)(2,1)S(1)} %get-tuple-element.56), channel_id=1, source_target_pairs={{0,16},{16,32},{32,48},{48,64},{64,80},{80,96},{96,112},{112,128},... | collective-permute-start | bytes 786440 | tf_op jit(solution)/shard_map/ppermute | solution.py:16
  136.7 0.9 copy-start.6
  137.6 2.0 copy-start.7
  137.6 8.9 %collective-permute-start.10 = (bf16[128,32,8]{0,2,1:T(8,128)(2,1)S(1)}, bf16[128,32,8]{0,2,1:T(8,128)(2,1)S(1)}, u32[]{:S(2)}, u32[]{:S(2)}) collective-permute-start(bf16[128,32,8]{0,2,1:T(8,128)(2,1)S(1)} %get-tuple-element.25), channel_id=1, source_target_pairs={{1,0},{2,1},{3,2},{4,3},{5,4},{6,5},{7,6},{8,7},{9,8},{10,9},{11,1... | collective-permute-start | bytes 196616 | tf_op jit(solution)/shard_map/ppermute | solution.py:17
  139.5 7.0 %collective-permute-start.11 = (bf16[128,32,8]{0,2,1:T(8,128)(2,1)S(1)}, bf16[128,32,8]{0,2,1:T(8,128)(2,1)S(1)}, u32[]{:S(2)}, u32[]{:S(2)}) collective-permute-start(bf16[128,32,8]{0,2,1:T(8,128)(2,1)S(1)} %get-tuple-element.24), channel_id=1, source_target_pairs={{0,1},{1,2},{2,3},{3,4},{4,5},{5,6},{6,7},{7,8},{8,9},{9,10},{10,1... | collective-permute-start | bytes 196616 | tf_op jit(solution)/shard_map/ppermute | solution.py:16
  148.9 5.2 copy-start.3
  155.3 8.1 %copy-start.5 = (bf16[128,2048]{1,0:T(8,128)(2,1)S(1)}, bf16[128,2048]{1,0:T(8,128)(2,1)}, u32[]{:S(2)}) copy-start(bf16[128,2048]{1,0:T(8,128)(2,1)} %copy-done.4) | copy-start | bytes 1572868
  178.7 11.1 %collective-permute-start.13 = (bf16[128,4,128]{0,1,2:T(4,128)(2,1)S(1)}, bf16[128,4,128]{0,1,2:T(4,128)(2,1)S(1)}, u32[]{:S(2)}, u32[]{:S(2)}) collective-permute-start(bf16[128,4,128]{0,1,2:T(4,128)(2,1)S(1)} %get-tuple-element.53), channel_id=1, source_target_pairs={{16,0},{32,16},{48,32},{64,48},{80,64},{96,80},{112,96},{128,112},... | collective-permute-start | bytes 393224 | tf_op jit(solution)/shard_map/ppermute | solution.py:17
  180.0 9.8 %collective-permute-start.12 = (bf16[128,4,128]{0,1,2:T(4,128)(2,1)S(1)}, bf16[128,4,128]{0,1,2:T(4,128)(2,1)S(1)}, u32[]{:S(2)}, u32[]{:S(2)}) collective-permute-start(bf16[128,4,128]{0,1,2:T(4,128)(2,1)S(1)} %get-tuple-element.52), channel_id=1, source_target_pairs={{0,16},{16,32},{32,48},{48,64},{64,80},{80,96},{96,112},{112,128},... | collective-permute-start | bytes 393224 | tf_op jit(solution)/shard_map/ppermute | solution.py:16
  189.9 6.9 %collective-permute-start.14 = (bf16[128,24,4]{0,1,2:T(8,128)(2,1)S(1)}, bf16[128,24,4]{0,1,2:T(8,128)(2,1)S(1)}, u32[]{:S(2)}, u32[]{:S(2)}) collective-permute-start(bf16[128,24,4]{0,1,2:T(8,128)(2,1)S(1)} %get-tuple-element.45), channel_id=1, source_target_pairs={{1,0},{2,1},{3,2},{4,3},{5,4},{6,5},{7,6},{8,7},{9,8},{10,9},{11,1... | collective-permute-start | bytes 73736 | tf_op jit(solution)/shard_map/ppermute | solution.py:17
  192.7 5.1 collective-permute-start.15
  207.0 12.8 %copy-start.8 = (bf16[128,16,128]{2,1,0:T(8,128)(2,1)S(1)}, bf16[128,16,128]{2,1,0:T(8,128)(2,1)}, u32[]{:S(2)}) copy-start(bf16[128,16,128]{2,1,0:T(8,128)(2,1)} %get-tuple-element.50) | copy-start | bytes 1572868
  221.6 132.1 %copy-start.10 = (bf16[128,2048]{1,0:T(8,128)(2,1)S(1)}, bf16[128,2048]{1,0:T(8,128)(2,1)}, u32[]{:S(2)}) copy-start(bf16[128,2048]{1,0:T(8,128)(2,1)} %copy-done.9) | copy-start | bytes 1572868
  221.6 308.9 %copy-start.1 = (bf16[128,768]{1,0:T(8,128)(2,1)S(1)}, bf16[128,768]{1,0:T(8,128)(2,1)}, u32[]{:S(2)}) copy-start(bf16[128,768]{1,0:T(8,128)(2,1)} %param.8) | copy-start | bytes 589828
  227.9 297.0 %all-reduce.5.cloned.1.call-start = ((), (), s32[]{:S(2)}) async-start(), calls=%async_computation | async-start | bytes 3145728 | tf_op jit(solution)/shard_map/psum | solution.py:102
Sparse Core Ops, SparseCore 0:
  228.0 125.6 all-reduce.6
  357.4 167.4 all-reduce.4
